TPU v7x, 256 devices: a whole 4x4x8 slice. The times are simulated.
256 devices in a mesh: grp: 8 (over x, core), lx: 4 (over y), ly: 8 (over z).
Axes of the slice: x: 4, y: 4, z: 8, core: 2. Of those that a mesh axis runs over, the one named last changes fastest.
Arguments:
- vectors: float32 [32, 256, 4096], P('grp', 'lx', 'ly'), may hold values from -6 to 6
- levels: int32 [256, 4096], P('lx', 'ly'), may hold values from 0 to 7
- level_table: float32 [8], replicated, may hold values from 1 to 3
- filter_low: float32 [1], replicated, may hold values from -1 to 0.5
- filter_high: float32 [1], replicated, may hold values from 6 to 7.5
Outputs:
- basis: float32 [32, 256, 4096], P('grp', 'lx', 'ly')
All inputs are finite; a program needn't handle non-finite values.
Results may differ from a plain program's by a relative error of at most 0.00011.
Values sent between devices are 32-bit elements; how exact they have to be, the bound alone decides.
No kernel may reach another device: no remote copies, remote signals or barrier semaphores. Data moves between devices by JAX's collectives and lax.ppermute only.
A program may use at most 64 MiB of HBM per device.

v0:
```python
import jax
import jax.numpy as jnp
from jax import lax
from jax.sharding import PartitionSpec as P


def padded_2(shard, sides, width):
    for axis, dim in sides:
        size, length = (lax.axis_size(axis), shard.shape[dim])
        up = [(i, (i + 1) % size) for i in range(size)]
        down = [(j, i) for i, j in up]
        last = lax.slice_in_dim(shard, length - width, length, axis=dim)
        leading = lax.slice_in_dim(shard, 0, width, axis=dim)
        before = lax.ppermute(last, axis, up)
        after = lax.ppermute(leading, axis, down)
        shard = jnp.concatenate([before, shard, after], axis=dim)
    return shard


def from_root(value, axis, source):
    kept = jnp.where(lax.axis_index(axis) == source, value, 0).astype(value.dtype)
    return lax.psum(kept, axis)


def apply_operator(field, onsite):
    padded = padded_2(field, (("lx", 1), ("ly", 2)), 1)
    beside = padded[:, 2:, 1:-1] + padded[:, :-2, 1:-1] + padded[:, 1:-1, 2:] + padded[:, 1:-1, :-2]
    return onsite[None] * field - beside


def lower_inverse(gram):
    lower = jnp.linalg.cholesky(gram)
    eye_block = jnp.eye(gram.shape[0], dtype=jnp.float32)
    return lax.linalg.triangular_solve(lower, eye_block, left_side=True, lower=True)


def body(vectors, levels, level_table, filter_low, filter_high):
    count_vec, rows_local, cols_local = vectors.shape
    level_ids = jnp.arange(level_table.shape[0], dtype=jnp.int32)
    onsite = jnp.sum(
        jnp.where(levels[None] == level_ids[:, None, None], level_table[:, None, None], 0.0), axis=0
    )
    center = (filter_high[0] + filter_low[0]) / 2.0
    half = (filter_high[0] - filter_low[0]) / 2.0
    first = (apply_operator(vectors, onsite) - center * vectors) / half
    filtered = 2.0 * (apply_operator(first, onsite) - center * first) / half - vectors
    total = rows_local * cols_local * lax.axis_size("lx") * lax.axis_size("ly")
    flat = filtered.reshape(count_vec, rows_local * cols_local)
    highest = lax.Precision.HIGHEST
    mine = lax.axis_index("grp")
    result = jnp.zeros_like(flat)
    for h in range(lax.axis_size("grp")):
        gram = lax.psum(jnp.dot(flat, flat.T, precision=highest), ("lx", "ly")) / total
        done = jnp.dot(lower_inverse(gram), flat, precision=highest)
        result = jnp.where(mine == h, done, result)
        shared = from_root(done, "grp", h)
        coeff = lax.psum(jnp.dot(shared, flat.T, precision=highest), ("lx", "ly")) / total
        later = mine > h
        flat = jnp.where(later, flat - jnp.dot(coeff.T, shared, precision=highest), flat)
    return result.reshape(count_vec, rows_local, cols_local)


def solution(mesh):
    in_specs = (P("grp", "lx", "ly"), P("lx", "ly"), P(), P(), P())
    out_specs = P("grp", "lx", "ly")
    return jax.shard_map(body, mesh=mesh, in_specs=in_specs, out_specs=out_specs, check_vma=False)
```

profile of v0, /device:TPU:32, one launch (start us, length us, event | category | flops | bytes accessed | tf_op | source)
XLA Modules:
  0.0 1632.8 jit_solution(7607256732290742390)
XLA Ops:
  7.4 3.1 collective-permute-start
  11.9 3.5 collective-permute-done.1
  21.7 3.9 collective-permute-done.3
  26.2 2.0 collective-permute-start.5
  31.3 3.3 collective-permute-start.6
  34.6 2.7 collective-permute-done.6
  37.3 2.5 collective-permute-done.7
  40.2 2.4 convolution_bitcast_fusion
  42.6 71.0 %psum.154 = f32[4,4]{0,1:T(4,128)S(1)} all-reduce(f32[4,4]{0,1:T(4,128)S(1)} %convolution_bitcast_fusion), channel_id=1, replica_groups=mesh['grp'=8,'lx'=4,'ly'=8] {'lx','ly'}, use_global_device_ids=true, to_apply=%region_1.2 | all-reduce | flops 16 | bytes 128 | tf_op jit(solution)/shard_map/psum | solution.py:53
  118.3 60.3 %all-reduce.8.cloned.1.call-done = f32[4,32768]{1,0:T(4,128)} async-done(((f32[4,32768]{1,0:T(4,128)}), f32[4,32768]{1,0:T(4,128)}) %all-reduce.8.cloned.1.call-update) | async-done | bytes 524304 | tf_op jit(solution)/shard_map/psum | solution.py:22
  178.6 3.5 fusion.99
  182.1 71.6 %psum.156 = f32[4,4]{0,1:T(4,128)S(1)} all-reduce(f32[4,4]{0,1:T(4,128)S(1)} %fusion.99), channel_id=1, replica_groups=mesh['grp'=8,'lx'=4,'ly'=8] {'lx','ly'}, use_global_device_ids=true, to_apply=%region_5.8 | all-reduce | flops 16 | bytes 128 | tf_op jit(solution)/shard_map/psum | solution.py:57
  254.8 2.3 fusion.100
  257.1 73.6 %psum.157 = f32[4,4]{0,1:T(4,128)S(1)} all-reduce(f32[4,4]{0,1:T(4,128)S(1)} %fusion.100), channel_id=1, replica_groups=mesh['grp'=8,'lx'=4,'ly'=8] {'lx','ly'}, use_global_device_ids=true, to_apply=%region_6.9 | all-reduce | flops 16 | bytes 128 | tf_op jit(solution)/shard_map/psum | solution.py:53
  335.0 58.1 %all-reduce.10.cloned.1.call-done = f32[4,32768]{1,0:T(4,128)} async-done(((f32[4,32768]{1,0:T(4,128)}), f32[4,32768]{1,0:T(4,128)}) %all-reduce.10.cloned.1.call-update) | async-done | bytes 524304 | tf_op jit(solution)/shard_map/psum | solution.py:22
  393.1 3.5 fusion.101
  396.6 71.6 %psum.159 = f32[4,4]{0,1:T(4,128)S(1)} all-reduce(f32[4,4]{0,1:T(4,128)S(1)} %fusion.101), channel_id=1, replica_groups=mesh['grp'=8,'lx'=4,'ly'=8] {'lx','ly'}, use_global_device_ids=true, to_apply=%region_8.11 | all-reduce | flops 16 | bytes 128 | tf_op jit(solution)/shard_map/psum | solution.py:57
  469.2 2.3 fusion.102
  471.6 73.6 %psum.160 = f32[4,4]{0,1:T(4,128)S(1)} all-reduce(f32[4,4]{0,1:T(4,128)S(1)} %fusion.102), channel_id=1, replica_groups=mesh['grp'=8,'lx'=4,'ly'=8] {'lx','ly'}, use_global_device_ids=true, to_apply=%region_9.12 | all-reduce | flops 16 | bytes 128 | tf_op jit(solution)/shard_map/psum | solution.py:53
  549.8 57.8 %all-reduce.12.cloned.1.call-done = f32[4,32768]{1,0:T(4,128)} async-done(((f32[4,32768]{1,0:T(4,128)}), f32[4,32768]{1,0:T(4,128)}) %all-reduce.12.cloned.1.call-update) | async-done | bytes 524304 | tf_op jit(solution)/shard_map/psum | solution.py:22
  607.6 3.5 fusion.103
  611.1 71.6 %psum.162 = f32[4,4]{0,1:T(4,128)S(1)} all-reduce(f32[4,4]{0,1:T(4,128)S(1)} %fusion.103), channel_id=1, replica_groups=mesh['grp'=8,'lx'=4,'ly'=8] {'lx','ly'}, use_global_device_ids=true, to_apply=%region_11.14 | all-reduce | flops 16 | bytes 128 | tf_op jit(solution)/shard_map/psum | solution.py:57
  683.7 2.3 fusion.104
  686.1 73.6 %psum.163 = f32[4,4]{0,1:T(4,128)S(1)} all-reduce(f32[4,4]{0,1:T(4,128)S(1)} %fusion.104), channel_id=1, replica_groups=mesh['grp'=8,'lx'=4,'ly'=8] {'lx','ly'}, use_global_device_ids=true, to_apply=%region_12.15 | all-reduce | flops 16 | bytes 128 | tf_op jit(solution)/shard_map/psum | solution.py:53
  764.0 58.1 %all-reduce.14.cloned.1.call-done = f32[4,32768]{1,0:T(4,128)} async-done(((f32[4,32768]{1,0:T(4,128)}), f32[4,32768]{1,0:T(4,128)}) %all-reduce.14.cloned.1.call-update) | async-done | bytes 524304 | tf_op jit(solution)/shard_map/psum | solution.py:22
  822.1 3.5 fusion.105
  825.6 71.6 %psum.165 = f32[4,4]{0,1:T(4,128)S(1)} all-reduce(f32[4,4]{0,1:T(4,128)S(1)} %fusion.105), channel_id=1, replica_groups=mesh['grp'=8,'lx'=4,'ly'=8] {'lx','ly'}, use_global_device_ids=true, to_apply=%region_14.17 | all-reduce | flops 16 | bytes 128 | tf_op jit(solution)/shard_map/psum | solution.py:57
  898.2 2.3 fusion.106
  900.6 73.6 %psum.166 = f32[4,4]{0,1:T(4,128)S(1)} all-reduce(f32[4,4]{0,1:T(4,128)S(1)} %fusion.106), channel_id=1, replica_groups=mesh['grp'=8,'lx'=4,'ly'=8] {'lx','ly'}, use_global_device_ids=true, to_apply=%region_15.18 | all-reduce | flops 16 | bytes 128 | tf_op jit(solution)/shard_map/psum | solution.py:53
  978.9 57.6 %all-reduce.16.cloned.1.call-done = f32[4,32768]{1,0:T(4,128)} async-done(((f32[4,32768]{1,0:T(4,128)}), f32[4,32768]{1,0:T(4,128)}) %all-reduce.16.cloned.1.call-update) | async-done | bytes 524304 | tf_op jit(solution)/shard_map/psum | solution.py:22
  1036.6 3.5 fusion.107
  1040.0 71.6 %psum.168 = f32[4,4]{0,1:T(4,128)S(1)} all-reduce(f32[4,4]{0,1:T(4,128)S(1)} %fusion.107), channel_id=1, replica_groups=mesh['grp'=8,'lx'=4,'ly'=8] {'lx','ly'}, use_global_device_ids=true, to_apply=%region_17.20 | all-reduce | flops 16 | bytes 128 | tf_op jit(solution)/shard_map/psum | solution.py:57
  1111.6 2.0 fusion.2
  1113.7 2.3 fusion.108
  1116.0 73.6 %psum.169 = f32[4,4]{0,1:T(4,128)S(1)} all-reduce(f32[4,4]{0,1:T(4,128)S(1)} %fusion.108), channel_id=1, replica_groups=mesh['grp'=8,'lx'=4,'ly'=8] {'lx','ly'}, use_global_device_ids=true, to_apply=%region_18.21 | all-reduce | flops 16 | bytes 128 | tf_op jit(solution)/shard_map/psum | solution.py:53
  1192.1 2.0 broadcast_select_fusion.1
  1194.2 58.1 %all-reduce.18.cloned.1.call-done = f32[4,32768]{1,0:T(4,128)} async-done(((f32[4,32768]{1,0:T(4,128)}), f32[4,32768]{1,0:T(4,128)}) %all-reduce.18.cloned.1.call-update) | async-done | bytes 524304 | tf_op jit(solution)/shard_map/psum | solution.py:22
  1252.2 3.5 fusion.109
  1255.7 71.6 %psum.171 = f32[4,4]{0,1:T(4,128)S(1)} all-reduce(f32[4,4]{0,1:T(4,128)S(1)} %fusion.109), channel_id=1, replica_groups=mesh['grp'=8,'lx'=4,'ly'=8] {'lx','ly'}, use_global_device_ids=true, to_apply=%region_20.23 | all-reduce | flops 16 | bytes 128 | tf_op jit(solution)/shard_map/psum | solution.py:57
  1327.3 2.0 fusion.1
  1329.3 2.3 fusion.110
  1331.6 73.8 %psum.172 = f32[4,4]{0,1:T(4,128)S(1)} all-reduce(f32[4,4]{0,1:T(4,128)S(1)} %fusion.110), channel_id=1, replica_groups=mesh['grp'=8,'lx'=4,'ly'=8] {'lx','ly'}, use_global_device_ids=true, to_apply=%region_21.24 | all-reduce | flops 16 | bytes 128 | tf_op jit(solution)/shard_map/psum | solution.py:53
  1409.9 58.1 %all-reduce.20.cloned.1.call-done = f32[4,32768]{1,0:T(4,128)} async-done(((f32[4,32768]{1,0:T(4,128)}), f32[4,32768]{1,0:T(4,128)}) %all-reduce.20.cloned.1.call-update) | async-done | bytes 524304 | tf_op jit(solution)/shard_map/psum | solution.py:22
  1468.0 3.5 fusion.111
  1471.5 71.6 %psum.174 = f32[4,4]{0,1:T(4,128)S(1)} all-reduce(f32[4,4]{0,1:T(4,128)S(1)} %fusion.111), channel_id=1, replica_groups=mesh['grp'=8,'lx'=4,'ly'=8] {'lx','ly'}, use_global_device_ids=true, to_apply=%region_23.26 | all-reduce | flops 16 | bytes 128 | tf_op jit(solution)/shard_map/psum | solution.py:57
  1543.1 2.0 fusion
  1545.1 2.3 fusion.112
  1547.5 73.6 %psum.175 = f32[4,4]{0,1:T(4,128)S(1)} all-reduce(f32[4,4]{0,1:T(4,128)S(1)} %fusion.112), channel_id=1, replica_groups=mesh['grp'=8,'lx'=4,'ly'=8] {'lx','ly'}, use_global_device_ids=true, to_apply=%region_24.27 | all-reduce | flops 16 | bytes 128 | tf_op jit(solution)/shard_map/psum | solution.py:53
  (131 shorter events, 49.7 us)
Async XLA Ops:
  6.5 172.1 %all-reduce.8.cloned.1.call-start = ((), (), s32[]{:S(2)}) async-start(), calls=%async_computation | async-start | bytes 1048576 | tf_op jit(solution)/shard_map/psum | solution.py:22
  7.4 4.5 collective-permute-start
  10.5 8.1 copy-start.6
  10.5 15.1 copy-start
  10.5 4.9 collective-permute-start.1
  16.5 2.1 copy-start.7
  16.5 5.2 collective-permute-start.2
  16.7 9.0 collective-permute-start.3
  26.1 3.7 collective-permute-start.4
  26.2 4.9 collective-permute-start.5
  31.3 6.0 collective-permute-start.6
  34.6 5.1 collective-permute-start.7
  118.0 275.1 %all-reduce.10.cloned.1.call-start = ((), (), s32[]{:S(2)}) async-start(), calls=%async_computation.1 | async-start | bytes 1048576 | tf_op jit(solution)/shard_map/psum | solution.py:22
  178.6 75.1 %copy-start.5 = (f32[4,32768]{1,0:T(4,128)S(1)}, f32[4,32768]{1,0:T(4,128)}, u32[]{:S(2)}) copy-start(f32[4,32768]{1,0:T(4,128)} %all-reduce.8.cloned.1.call-done) | copy-start | bytes 1572868
  335.0 272.6 %all-reduce.12.cloned.1.call-start = ((), (), s32[]{:S(2)}) async-start(), calls=%async_computation.2 | async-start | bytes 1048576 | tf_op jit(solution)/shard_map/psum | solution.py:22
  393.1 75.1 %copy-start.2 = (f32[4,32768]{1,0:T(4,128)S(1)}, f32[4,32768]{1,0:T(4,128)}, u32[]{:S(2)}) copy-start(f32[4,32768]{1,0:T(4,128)} %all-reduce.10.cloned.1.call-done) | copy-start | bytes 1572868
  549.5 272.6 %all-reduce.14.cloned.1.call-start = ((), (), s32[]{:S(2)}) async-start(), calls=%async_computation.3 | async-start | bytes 1048576 | tf_op jit(solution)/shard_map/psum | solution.py:22
  607.6 75.1 %copy-start.3 = (f32[4,32768]{1,0:T(4,128)S(1)}, f32[4,32768]{1,0:T(4,128)}, u32[]{:S(2)}) copy-start(f32[4,32768]{1,0:T(4,128)} %all-reduce.12.cloned.1.call-done) | copy-start | bytes 1572868
  764.0 272.6 %all-reduce.16.cloned.1.call-start = ((), (), s32[]{:S(2)}) async-start(), calls=%async_computation.4 | async-start | bytes 1048576 | tf_op jit(solution)/shard_map/psum | solution.py:22
  822.1 75.1 %copy-start.4 = (f32[4,32768]{1,0:T(4,128)S(1)}, f32[4,32768]{1,0:T(4,128)}, u32[]{:S(2)}) copy-start(f32[4,32768]{1,0:T(4,128)} %all-reduce.14.cloned.1.call-done) | copy-start | bytes 1572868
  978.5 273.7 %all-reduce.18.cloned.1.call-start = ((), (), s32[]{:S(2)}) async-start(), calls=%async_computation.5 | async-start | bytes 1048576 | tf_op jit(solution)/shard_map/psum | solution.py:22
  1194.1 273.9 %all-reduce.20.cloned.1.call-start = ((), (), s32[]{:S(2)}) async-start(), calls=%async_computation.6 | async-start | bytes 1048576 | tf_op jit(solution)/shard_map/psum | solution.py:22
  1545.1 78.4 %copy-start.1 = (f32[4,32768]{1,0:T(4,128)S(1)}, f32[4,32768]{1,0:T(4,128)}, u32[]{:S(2)}) copy-start(f32[4,32768]{1,0:T(4,128)} %convolution_select_fusion.1) | copy-start | bytes 1572868
Sparse Core Ops, SparseCore 0:
  118.2 60.3 all-reduce.7
  335.1 57.9 all-reduce.9
  549.6 57.9 all-reduce.11
  764.1 57.9 all-reduce.13
  978.6 57.9 all-reduce.15
  1194.2 57.9 all-reduce.17
  1410.0 57.9 all-reduce.19
where the time goes:
time: 1640 us; the launch traced here: 1630 us
  blocking collectives  1090 us (66%)
  waiting for transfers between devices  427 us (26%)
  matrix products  69.2 us (4%)
  other arithmetic  19.4 us (1%)
    psum x8, blocking collectives, body(): lax.psum(jnp.dot(flat, flat.T, precision=highest), ('lx', 'ly')) / total  586 us
    psum x7, blocking collectives, body(): lax.psum(jnp.dot(shared, flat.T, precision=highest), ('lx', 'ly')) / total  501 us
    psum x7, waiting for transfers between devices, from_root(): return lax.psum(kept, axis)  408 us
  transfers between devices with their start and end apart: 15, of which 15 were waited for; matrix products, arithmetic and copies ran while one was open for 0% of the time, Pallas kernels for 0%

commit v1 on v0

--- a/solution.py
+++ b/solution.py
@@ -54,7 +54,12 @@
         done = jnp.dot(lower_inverse(gram), flat, precision=highest)
         result = jnp.where(mine == h, done, result)
         shared = from_root(done, "grp", h)
-        coeff = lax.psum(jnp.dot(shared, flat.T, precision=highest), ("lx", "ly")) / total
+        coeff = (
+            jnp.sum(
+                lax.all_gather(jnp.dot(shared, flat.T, precision=highest), ("lx", "ly")), axis=0
+            )
+            / total
+        )
         later = mine > h
         flat = jnp.where(later, flat - jnp.dot(coeff.T, shared, precision=highest), flat)
     return result.reshape(count_vec, rows_local, cols_local)

time: 1640 us -> 1470 us (0.90)
  blocking collectives: 1090 us -> 910 us
    psum x7 -> x0, blocking collectives: 501 us -> none  [body(): lax.psum(jnp.dot(shared, flat.T, precision=highest), ('lx', 'ly')) / total]
    all_gather x0 -> x7, blocking collectives: none -> 342 us  [body(): lax.all_gather(jnp.dot(shared, flat.T, precision=highest), ('lx', 'ly'))]
    psum x8, blocking collectives: 586 us -> 568 us  [body(): lax.psum(jnp.dot(flat, flat.T, precision=highest), ('lx', 'ly')) / total]
where the time goes in v1:
time: 1470 us; the launch traced here: 1460 us
  blocking collectives  910 us (62%)
  waiting for transfers between devices  433 us (29%)
  matrix products  69.8 us (5%)
  other arithmetic  19.7 us (1%)
  between operations  15.3 us (1%)
    psum x8, blocking collectives, body(): lax.psum(jnp.dot(flat, flat.T, precision=highest), ('lx', 'ly')) / total  568 us
    psum x7, waiting for transfers between devices, from_root(): return lax.psum(kept, axis)  415 us
    all_gather x7, blocking collectives, body(): lax.all_gather(jnp.dot(shared, flat.T, precision=highest), ('lx', 'ly'))  342 us
  transfers between devices with their start and end apart: 15, of which 15 were waited for; matrix products, arithmetic and copies ran while one was open for 0% of the time, Pallas kernels for 0%

profile of v1, /device:TPU:32, one launch (start us, length us, event | category | flops | bytes accessed | tf_op | source)
XLA Modules:
  0.0 1463.1 jit_solution(9946818929637149135)
XLA Ops:
  7.4 3.1 collective-permute-start
  11.9 3.5 collective-permute-done.1
  21.7 3.9 collective-permute-done.3
  26.2 2.0 collective-permute-start.5
  31.3 3.3 collective-permute-start.6
  34.6 2.7 collective-permute-done.6
  37.3 2.5 collective-permute-done.7
  40.2 2.4 convolution_bitcast_fusion.7
  42.6 71.0 %psum.105 = f32[4,4]{0,1:T(4,128)S(1)} all-reduce(f32[4,4]{0,1:T(4,128)S(1)} %convolution_bitcast_fusion.7), channel_id=1, replica_groups=mesh['grp'=8,'lx'=4,'ly'=8] {'lx','ly'}, use_global_device_ids=true, to_apply=%region_1.2 | all-reduce | flops 16 | bytes 128 | tf_op jit(solution)/shard_map/psum | solution.py:53
  118.3 60.3 %all-reduce.8.cloned.1.call-done = f32[4,32768]{1,0:T(4,128)} async-done(((f32[4,32768]{1,0:T(4,128)}), f32[4,32768]{1,0:T(4,128)}) %all-reduce.8.cloned.1.call-update) | async-done | bytes 524304 | tf_op jit(solution)/shard_map/psum | solution.py:22
  178.6 3.6 convolution_bitcast_fusion.6
  182.2 48.8 %all-gather.7 = f32[32,4,4]{2,1,0:T(4,128)S(1)} all-gather(f32[1,4,4]{2,1,0:T(4,128)S(1)} %convolution_bitcast_fusion.6), channel_id=2, replica_groups=mesh['grp'=8,'lx'=4,'ly'=8] {'lx','ly'}, dimensions={0}, use_global_device_ids=true | all-gather | bytes 2112 | tf_op jit(solution)/shard_map/all_gather | solution.py:59
  232.2 2.3 fusion.99
  234.5 71.0 %psum.107 = f32[4,4]{0,1:T(4,128)S(1)} all-reduce(f32[4,4]{0,1:T(4,128)S(1)} %fusion.99), channel_id=1, replica_groups=mesh['grp'=8,'lx'=4,'ly'=8] {'lx','ly'}, use_global_device_ids=true, to_apply=%region_6.9 | all-reduce | flops 16 | bytes 128 | tf_op jit(solution)/shard_map/psum | solution.py:53
  309.9 59.2 %all-reduce.10.cloned.1.call-done = f32[4,32768]{1,0:T(4,128)} async-done(((f32[4,32768]{1,0:T(4,128)}), f32[4,32768]{1,0:T(4,128)}) %all-reduce.10.cloned.1.call-update) | async-done | bytes 524304 | tf_op jit(solution)/shard_map/psum | solution.py:22
  369.0 3.6 convolution_bitcast_fusion.5
  372.6 48.8 %all-gather.8 = f32[32,4,4]{2,1,0:T(4,128)S(1)} all-gather(f32[1,4,4]{2,1,0:T(4,128)S(1)} %convolution_bitcast_fusion.5), channel_id=3, replica_groups=mesh['grp'=8,'lx'=4,'ly'=8] {'lx','ly'}, dimensions={0}, use_global_device_ids=true | all-gather | bytes 2112 | tf_op jit(solution)/shard_map/all_gather | solution.py:59
  422.6 2.3 fusion.100
  424.9 71.0 %psum.109 = f32[4,4]{0,1:T(4,128)S(1)} all-reduce(f32[4,4]{0,1:T(4,128)S(1)} %fusion.100), channel_id=1, replica_groups=mesh['grp'=8,'lx'=4,'ly'=8] {'lx','ly'}, use_global_device_ids=true, to_apply=%region_9.12 | all-reduce | flops 16 | bytes 128 | tf_op jit(solution)/shard_map/psum | solution.py:53
  500.5 59.0 %all-reduce.12.cloned.1.call-done = f32[4,32768]{1,0:T(4,128)} async-done(((f32[4,32768]{1,0:T(4,128)}), f32[4,32768]{1,0:T(4,128)}) %all-reduce.12.cloned.1.call-update) | async-done | bytes 524304 | tf_op jit(solution)/shard_map/psum | solution.py:22
  559.4 3.6 convolution_bitcast_fusion.4
  563.0 48.8 %all-gather.9 = f32[32,4,4]{2,1,0:T(4,128)S(1)} all-gather(f32[1,4,4]{2,1,0:T(4,128)S(1)} %convolution_bitcast_fusion.4), channel_id=4, replica_groups=mesh['grp'=8,'lx'=4,'ly'=8] {'lx','ly'}, dimensions={0}, use_global_device_ids=true | all-gather | bytes 2112 | tf_op jit(solution)/shard_map/all_gather | solution.py:59
  613.0 2.3 fusion.101
  615.3 71.0 %psum.111 = f32[4,4]{0,1:T(4,128)S(1)} all-reduce(f32[4,4]{0,1:T(4,128)S(1)} %fusion.101), channel_id=1, replica_groups=mesh['grp'=8,'lx'=4,'ly'=8] {'lx','ly'}, use_global_device_ids=true, to_apply=%region_12.15 | all-reduce | flops 16 | bytes 128 | tf_op jit(solution)/shard_map/psum | solution.py:53
  690.7 59.2 %all-reduce.14.cloned.1.call-done = f32[4,32768]{1,0:T(4,128)} async-done(((f32[4,32768]{1,0:T(4,128)}), f32[4,32768]{1,0:T(4,128)}) %all-reduce.14.cloned.1.call-update) | async-done | bytes 524304 | tf_op jit(solution)/shard_map/psum | solution.py:22
  749.8 3.6 convolution_bitcast_fusion.3
  753.4 48.8 %all-gather.10 = f32[32,4,4]{2,1,0:T(4,128)S(1)} all-gather(f32[1,4,4]{2,1,0:T(4,128)S(1)} %convolution_bitcast_fusion.3), channel_id=5, replica_groups=mesh['grp'=8,'lx'=4,'ly'=8] {'lx','ly'}, dimensions={0}, use_global_device_ids=true | all-gather | bytes 2112 | tf_op jit(solution)/shard_map/all_gather | solution.py:59
  803.4 2.3 fusion.102
  805.7 71.0 %psum.113 = f32[4,4]{0,1:T(4,128)S(1)} all-reduce(f32[4,4]{0,1:T(4,128)S(1)} %fusion.102), channel_id=1, replica_groups=mesh['grp'=8,'lx'=4,'ly'=8] {'lx','ly'}, use_global_device_ids=true, to_apply=%region_15.18 | all-reduce | flops 16 | bytes 128 | tf_op jit(solution)/shard_map/psum | solution.py:53
  881.5 58.8 %all-reduce.16.cloned.1.call-done = f32[4,32768]{1,0:T(4,128)} async-done(((f32[4,32768]{1,0:T(4,128)}), f32[4,32768]{1,0:T(4,128)}) %all-reduce.16.cloned.1.call-update) | async-done | bytes 524304 | tf_op jit(solution)/shard_map/psum | solution.py:22
  940.2 3.5 convolution_bitcast_fusion.2
  943.7 48.8 %all-gather.11 = f32[32,4,4]{2,1,0:T(4,128)S(1)} all-gather(f32[1,4,4]{2,1,0:T(4,128)S(1)} %convolution_bitcast_fusion.2), channel_id=6, replica_groups=mesh['grp'=8,'lx'=4,'ly'=8] {'lx','ly'}, dimensions={0}, use_global_device_ids=true | all-gather | bytes 2112 | tf_op jit(solution)/shard_map/all_gather | solution.py:59
  992.7 2.0 fusion.2
  994.7 2.3 fusion.103
  997.1 71.0 %psum.115 = f32[4,4]{0,1:T(4,128)S(1)} all-reduce(f32[4,4]{0,1:T(4,128)S(1)} %fusion.103), channel_id=1, replica_groups=mesh['grp'=8,'lx'=4,'ly'=8] {'lx','ly'}, use_global_device_ids=true, to_apply=%region_18.21 | all-reduce | flops 16 | bytes 128 | tf_op jit(solution)/shard_map/psum | solution.py:53
  1070.5 2.0 broadcast_select_fusion.1
  1072.6 59.2 %all-reduce.18.cloned.1.call-done = f32[4,32768]{1,0:T(4,128)} async-done(((f32[4,32768]{1,0:T(4,128)}), f32[4,32768]{1,0:T(4,128)}) %all-reduce.18.cloned.1.call-update) | async-done | bytes 524304 | tf_op jit(solution)/shard_map/psum | solution.py:22
  1131.8 3.5 convolution_bitcast_fusion.1
  1135.3 48.8 %all-gather.12 = f32[32,4,4]{2,1,0:T(4,128)S(1)} all-gather(f32[1,4,4]{2,1,0:T(4,128)S(1)} %convolution_bitcast_fusion.1), channel_id=7, replica_groups=mesh['grp'=8,'lx'=4,'ly'=8] {'lx','ly'}, dimensions={0}, use_global_device_ids=true | all-gather | bytes 2112 | tf_op jit(solution)/shard_map/all_gather | solution.py:59
  1184.2 2.0 fusion.1
  1186.3 2.3 fusion.104
  1188.6 71.2 %psum.117 = f32[4,4]{0,1:T(4,128)S(1)} all-reduce(f32[4,4]{0,1:T(4,128)S(1)} %fusion.104), channel_id=1, replica_groups=mesh['grp'=8,'lx'=4,'ly'=8] {'lx','ly'}, use_global_device_ids=true, to_apply=%region_21.24 | all-reduce | flops 16 | bytes 128 | tf_op jit(solution)/shard_map/psum | solution.py:53
  1264.3 59.3 %all-reduce.20.cloned.1.call-done = f32[4,32768]{1,0:T(4,128)} async-done(((f32[4,32768]{1,0:T(4,128)}), f32[4,32768]{1,0:T(4,128)}) %all-reduce.20.cloned.1.call-update) | async-done | bytes 524304 | tf_op jit(solution)/shard_map/psum | solution.py:22
  1323.5 3.5 convolution_bitcast_fusion
  1327.1 48.8 %all-gather.13 = f32[32,4,4]{2,1,0:T(4,128)S(1)} all-gather(f32[1,4,4]{2,1,0:T(4,128)S(1)} %convolution_bitcast_fusion), channel_id=8, replica_groups=mesh['grp'=8,'lx'=4,'ly'=8] {'lx','ly'}, dimensions={0}, use_global_device_ids=true | all-gather | bytes 2112 | tf_op jit(solution)/shard_map/all_gather | solution.py:59
  1376.0 2.0 fusion
  1378.0 2.3 fusion.105
  1380.4 71.0 %psum.119 = f32[4,4]{0,1:T(4,128)S(1)} all-reduce(f32[4,4]{0,1:T(4,128)S(1)} %fusion.105), channel_id=1, replica_groups=mesh['grp'=8,'lx'=4,'ly'=8] {'lx','ly'}, use_global_device_ids=true, to_apply=%region_24.27 | all-reduce | flops 16 | bytes 128 | tf_op jit(solution)/shard_map/psum | solution.py:53
  (145 shorter events, 50.7 us)
Async XLA Ops:
  6.5 172.1 %all-reduce.8.cloned.1.call-start = ((), (), s32[]{:S(2)}) async-start(), calls=%async_computation | async-start | bytes 1048576 | tf_op jit(solution)/shard_map/psum | solution.py:22
  7.4 4.5 collective-permute-start
  10.5 8.1 copy-start.6
  10.5 15.1 %copy-start = (f32[4,64,512]{2,1,0:T(8,128)S(1)}, f32[4,64,512]{2,1,0:T(8,128)}, u32[]{:S(2)}) copy-start(f32[4,64,512]{2,1,0:T(8,128)} %param.8) | copy-start | bytes 1572868
  10.5 4.9 collective-permute-start.1
  16.5 2.1 copy-start.7
  16.5 5.2 collective-permute-start.2
  16.7 9.0 collective-permute-start.3
  26.1 3.7 collective-permute-start.4
  26.2 4.9 collective-permute-start.5
  31.3 6.0 collective-permute-start.6
  34.6 5.1 collective-permute-start.7
  118.0 251.0 %all-reduce.10.cloned.1.call-start = ((), (), s32[]{:S(2)}) async-start(), calls=%async_computation.1 | async-start | bytes 1048576 | tf_op jit(solution)/shard_map/psum | solution.py:22
  178.6 52.5 %copy-start.5 = (f32[4,32768]{1,0:T(4,128)S(1)}, f32[4,32768]{1,0:T(4,128)}, u32[]{:S(2)}) copy-start(f32[4,32768]{1,0:T(4,128)} %all-reduce.8.cloned.1.call-done) | copy-start | bytes 1572868
  309.8 249.6 %all-reduce.12.cloned.1.call-start = ((), (), s32[]{:S(2)}) async-start(), calls=%async_computation.2 | async-start | bytes 1048576 | tf_op jit(solution)/shard_map/psum | solution.py:22
  369.0 52.5 %copy-start.2 = (f32[4,32768]{1,0:T(4,128)S(1)}, f32[4,32768]{1,0:T(4,128)}, u32[]{:S(2)}) copy-start(f32[4,32768]{1,0:T(4,128)} %all-reduce.10.cloned.1.call-done) | copy-start | bytes 1572868
  500.2 249.6 %all-reduce.14.cloned.1.call-start = ((), (), s32[]{:S(2)}) async-start(), calls=%async_computation.3 | async-start | bytes 1048576 | tf_op jit(solution)/shard_map/psum | solution.py:22
  559.4 52.5 %copy-start.3 = (f32[4,32768]{1,0:T(4,128)S(1)}, f32[4,32768]{1,0:T(4,128)}, u32[]{:S(2)}) copy-start(f32[4,32768]{1,0:T(4,128)} %all-reduce.12.cloned.1.call-done) | copy-start | bytes 1572868
  690.6 249.6 %all-reduce.16.cloned.1.call-start = ((), (), s32[]{:S(2)}) async-start(), calls=%async_computation.4 | async-start | bytes 1048576 | tf_op jit(solution)/shard_map/psum | solution.py:22
  749.8 52.5 %copy-start.4 = (f32[4,32768]{1,0:T(4,128)S(1)}, f32[4,32768]{1,0:T(4,128)}, u32[]{:S(2)}) copy-start(f32[4,32768]{1,0:T(4,128)} %all-reduce.14.cloned.1.call-done) | copy-start | bytes 1572868
  881.0 250.8 %all-reduce.18.cloned.1.call-start = ((), (), s32[]{:S(2)}) async-start(), calls=%async_computation.5 | async-start | bytes 1048576 | tf_op jit(solution)/shard_map/psum | solution.py:22
  1072.5 251.0 %all-reduce.20.cloned.1.call-start = ((), (), s32[]{:S(2)}) async-start(), calls=%async_computation.6 | async-start | bytes 1048576 | tf_op jit(solution)/shard_map/psum | solution.py:22
  1378.0 75.8 %copy-start.1 = (f32[4,32768]{1,0:T(4,128)S(1)}, f32[4,32768]{1,0:T(4,128)}, u32[]{:S(2)}) copy-start(f32[4,32768]{1,0:T(4,128)} %convolution_select_fusion.1) | copy-start | bytes 1572868
Sparse Core Ops, SparseCore 0:
  118.2 60.3 all-reduce.7
  309.9 59.0 all-reduce.9
  500.3 59.0 all-reduce.11
  690.7 59.0 all-reduce.13
  881.1 59.0 all-reduce.15
  1072.7 59.0 all-reduce.17
  1264.4 59.1 all-reduce.19
